TPU v7x, 128 devices: a whole 4x4x4 slice. The times are simulated.
128 devices in a mesh: row: 16 (over x_hi, y, core), col: 8 (over x_lo, z).
Axes of the slice: x: 4 (x_hi: 2, x_lo: 2; x = x_hi * 2 + x_lo), y: 4, z: 4, core: 2. Of those that a mesh axis runs over, the one named last changes fastest.
Arguments:
- points: bfloat16 [65536, 128], P(('row', 'col')), may hold values from -6 to 6
- probes: bfloat16 [65536, 128], P(('row', 'col')), may hold values from -6 to 6
Outputs:
- sketch: float32 [65536, 128], P(('row', 'col'))
- basis: float32 [65536, 128], P(('row', 'col'))
All inputs are finite; a program needn't handle non-finite values.
Results may differ from a plain program's by a relative error of at most 0.0044.
Values may be sent and summed in bfloat16 or wider, within the bound.
No kernel may reach another device: no remote copies, remote signals or barrier semaphores. Data moves between devices by JAX's collectives and lax.ppermute only.
A program may use at most 64 MiB of HBM per device.

v0:
```python
import math
import jax
import jax.numpy as jnp
from jax import lax
from jax.sharding import PartitionSpec as P


def shards(points, probes):
    own_count = points.shape[0]
    width = points.shape[1]
    nprobe = probes.shape[1]
    factor = -3.0 / width
    row_pts = lax.all_gather(points, "col", axis=0, tiled=True)
    row_sq = jnp.sum(jnp.square(row_pts.astype(jnp.float32)), axis=1)
    nrows = row_pts.shape[0]
    block = math.gcd(nrows, 512)
    nblocks = nrows // block
    blocked = row_pts.reshape(nblocks, block, width)
    sq_blocked = row_sq.reshape(nblocks, block)
    start_sum = jnp.zeros((nrows, nprobe), jnp.float32)
    col_pts = lax.all_gather(points, "row", axis=0, tiled=True)
    col_probe = lax.all_gather(probes, "row", axis=0, tiled=True)
    col_sq = jnp.sum(jnp.square(col_pts.astype(jnp.float32)), axis=1)

    def one_block(args):
        rows, sq_rows = args
        cross = lax.dot_general(
            rows, col_pts, (((1,), (1,)), ((), ())), preferred_element_type=jnp.float32
        )
        expo = (sq_rows[:, None] + col_sq[None, :] - 2.0 * cross) * factor
        kernel = jnp.exp(expo).astype(jnp.bfloat16)
        return jnp.dot(kernel, col_probe, preferred_element_type=jnp.float32)

    terms = lax.map(one_block, (blocked, sq_blocked))
    partial_rows = terms.reshape(nrows, start_sum.shape[1])
    total = lax.psum(partial_rows, "col")
    own_rows = lax.dynamic_slice_in_dim(total, lax.axis_index("col") * own_count, own_count, 0)
    all_points = own_count * lax.axis_size("row") * lax.axis_size("col")
    gram_part = jnp.dot(
        own_rows.T, own_rows, precision=lax.Precision.HIGHEST, preferred_element_type=jnp.float32
    )
    gram = lax.psum(gram_part, ("row", "col"))
    lower = jnp.linalg.cholesky(gram)
    solved = jax.scipy.linalg.solve_triangular(lower, own_rows.T, lower=True)
    basis = solved.T * math.sqrt(all_points)
    return (own_rows, basis)


def solution(mesh):
    in_specs = (P(("row", "col"), None), P(("row", "col"), None))
    out_specs = (P(("row", "col"), None), P(("row", "col"), None))
    return jax.shard_map(shards, mesh=mesh, in_specs=in_specs, out_specs=out_specs, check_vma=False)
```

profile of v0, /device:TPU:1, one launch (start us, length us, event | category | flops | bytes accessed | tf_op | source)
XLA Modules:
  0.0 462.9 jit_solution(4579630985239570801)
XLA Ops:
  7.2 0.0 all-gather.4.cloned.1.call-start
  7.2 0.7 all-gather.4.cloned.1.call-update
  7.9 0.0 all-gather.6.cloned.1.call-start
  7.9 0.7 all-gather.6.cloned.1.call-update
  8.6 0.0 all-gather.8.cloned.1.call-start
  8.7 0.7 all-gather.8.cloned.1.call-update
  9.4 0.0 all-reduce.3.cloned.1.call-start
  9.4 37.8 %all-gather.4.cloned.1.call-done = bf16[4096,128]{1,0:T(8,128)(2,1)} async-done(((bf16[512,128]{1,0:T(8,128)(2,1)}), bf16[4096,128]{1,0:T(8,128)(2,1)}) %all-gather.4.cloned.1.call-update) | async-done | bytes 1048592 | tf_op jit(solution)/shard_map/all_gather | solution.py:13
  47.2 1.8 multiply_reduce_fusion.1
  49.1 52.3 %all-gather.6.cloned.1.call-done = bf16[8192,128]{1,0:T(8,128)(2,1)} async-done(((bf16[512,128]{1,0:T(8,128)(2,1)}), bf16[8192,128]{1,0:T(8,128)(2,1)}) %all-gather.6.cloned.1.call-update) | async-done | bytes 2097168 | tf_op jit(solution)/shard_map/all_gather | solution.py:21
  101.4 0.0 copy-start.1
  101.4 2.9 multiply_reduce_fusion
  104.3 45.9 %all-gather.8.cloned.1.call-done = bf16[8192,128]{1,0:T(8,128)(2,1)} async-done(((bf16[512,128]{1,0:T(8,128)(2,1)}), bf16[8192,128]{1,0:T(8,128)(2,1)}) %all-gather.8.cloned.1.call-update) | async-done | bytes 2097168 | tf_op jit(solution)/shard_map/all_gather | solution.py:22
  150.2 0.0 copy-done.1
  150.2 56.3 %while.10 = (s32[]{:T(128)}, f32[8,512,128]{2,1,0:T(8,128)}, f32[8,512]{1,0:T(8,128)S(1)}, f32[8192]{0:T(1024)S(1)}, bf16[8,512,128]{2,1,0:T(8,128)(2,1)}, /*ind...) while((s32[]{:T(128)}, f32[8,512,128]{2,1,0:T(8,128)}, f32[8,512]{1,0:T(8,128)S(1)}, ...), condition=%wide.region_3.4_spmd, body=%wide.region_2.3_spmd.sunk | while | flops 2168455168 | bytes 4627545 | solution.py:34
  150.2 7.0 %fusion.27 = f32[8,512,128]{2,1,0:T(8,128)} fusion(f32[8,512,128]{2,1,0:T(8,128)} %get-tuple-element.106, s32[]{:T(128)} %get-tuple-element.105, bf16[8192,128]{1,0:T(8,128)(2,1)} %get-tuple-element.119, bf16[8192,128]{1,0:T(8,128)(2,1)S(1)} %get-tuple-element.118, f32[8192]{0:T(1024)S(1)} %get-tuple-element.116, f32[512]{0:T(512)S(1)} %bitcast.37, ...), kind=kOutput, calls=%fused_computation.3.clone.1 | convolution fusion | flops 2168455168 | bytes 4623360 | tf_op jit(solution)/shard_map/while/body/eval_jaxpr/dot_general | solution.py:32
  157.2 7.0 %fusion.27 = f32[8,512,128]{2,1,0:T(8,128)} fusion(f32[8,512,128]{2,1,0:T(8,128)} %get-tuple-element.106, s32[]{:T(128)} %get-tuple-element.105, bf16[8192,128]{1,0:T(8,128)(2,1)} %get-tuple-element.119, bf16[8192,128]{1,0:T(8,128)(2,1)S(1)} %get-tuple-element.118, f32[8192]{0:T(1024)S(1)} %get-tuple-element.116, f32[512]{0:T(512)S(1)} %bitcast.37, ...), kind=kOutput, calls=%fused_computation.3.clone.1 | convolution fusion | flops 2168455168 | bytes 4623360 | tf_op jit(solution)/shard_map/while/body/eval_jaxpr/dot_general | solution.py:32
  164.3 7.0 %fusion.27 = f32[8,512,128]{2,1,0:T(8,128)} fusion(f32[8,512,128]{2,1,0:T(8,128)} %get-tuple-element.106, s32[]{:T(128)} %get-tuple-element.105, bf16[8192,128]{1,0:T(8,128)(2,1)} %get-tuple-element.119, bf16[8192,128]{1,0:T(8,128)(2,1)S(1)} %get-tuple-element.118, f32[8192]{0:T(1024)S(1)} %get-tuple-element.116, f32[512]{0:T(512)S(1)} %bitcast.37, ...), kind=kOutput, calls=%fused_computation.3.clone.1 | convolution fusion | flops 2168455168 | bytes 4623360 | tf_op jit(solution)/shard_map/while/body/eval_jaxpr/dot_general | solution.py:32
  171.3 7.0 %fusion.27 = f32[8,512,128]{2,1,0:T(8,128)} fusion(f32[8,512,128]{2,1,0:T(8,128)} %get-tuple-element.106, s32[]{:T(128)} %get-tuple-element.105, bf16[8192,128]{1,0:T(8,128)(2,1)} %get-tuple-element.119, bf16[8192,128]{1,0:T(8,128)(2,1)S(1)} %get-tuple-element.118, f32[8192]{0:T(1024)S(1)} %get-tuple-element.116, f32[512]{0:T(512)S(1)} %bitcast.37, ...), kind=kOutput, calls=%fused_computation.3.clone.1 | convolution fusion | flops 2168455168 | bytes 4623360 | tf_op jit(solution)/shard_map/while/body/eval_jaxpr/dot_general | solution.py:32
  178.3 7.0 %fusion.27 = f32[8,512,128]{2,1,0:T(8,128)} fusion(f32[8,512,128]{2,1,0:T(8,128)} %get-tuple-element.106, s32[]{:T(128)} %get-tuple-element.105, bf16[8192,128]{1,0:T(8,128)(2,1)} %get-tuple-element.119, bf16[8192,128]{1,0:T(8,128)(2,1)S(1)} %get-tuple-element.118, f32[8192]{0:T(1024)S(1)} %get-tuple-element.116, f32[512]{0:T(512)S(1)} %bitcast.37, ...), kind=kOutput, calls=%fused_computation.3.clone.1 | convolution fusion | flops 2168455168 | bytes 4623360 | tf_op jit(solution)/shard_map/while/body/eval_jaxpr/dot_general | solution.py:32
  185.4 7.0 %fusion.27 = f32[8,512,128]{2,1,0:T(8,128)} fusion(f32[8,512,128]{2,1,0:T(8,128)} %get-tuple-element.106, s32[]{:T(128)} %get-tuple-element.105, bf16[8192,128]{1,0:T(8,128)(2,1)} %get-tuple-element.119, bf16[8192,128]{1,0:T(8,128)(2,1)S(1)} %get-tuple-element.118, f32[8192]{0:T(1024)S(1)} %get-tuple-element.116, f32[512]{0:T(512)S(1)} %bitcast.37, ...), kind=kOutput, calls=%fused_computation.3.clone.1 | convolution fusion | flops 2168455168 | bytes 4623360 | tf_op jit(solution)/shard_map/while/body/eval_jaxpr/dot_general | solution.py:32
  192.4 7.0 %fusion.27 = f32[8,512,128]{2,1,0:T(8,128)} fusion(f32[8,512,128]{2,1,0:T(8,128)} %get-tuple-element.106, s32[]{:T(128)} %get-tuple-element.105, bf16[8192,128]{1,0:T(8,128)(2,1)} %get-tuple-element.119, bf16[8192,128]{1,0:T(8,128)(2,1)S(1)} %get-tuple-element.118, f32[8192]{0:T(1024)S(1)} %get-tuple-element.116, f32[512]{0:T(512)S(1)} %bitcast.37, ...), kind=kOutput, calls=%fused_computation.3.clone.1 | convolution fusion | flops 2168455168 | bytes 4623360 | tf_op jit(solution)/shard_map/while/body/eval_jaxpr/dot_general | solution.py:32
  199.4 7.0 %fusion.27 = f32[8,512,128]{2,1,0:T(8,128)} fusion(f32[8,512,128]{2,1,0:T(8,128)} %get-tuple-element.106, s32[]{:T(128)} %get-tuple-element.105, bf16[8192,128]{1,0:T(8,128)(2,1)} %get-tuple-element.119, bf16[8192,128]{1,0:T(8,128)(2,1)S(1)} %get-tuple-element.118, f32[8192]{0:T(1024)S(1)} %get-tuple-element.116, f32[512]{0:T(512)S(1)} %bitcast.37, ...), kind=kOutput, calls=%fused_computation.3.clone.1 | convolution fusion | flops 2168455168 | bytes 4623360 | tf_op jit(solution)/shard_map/while/body/eval_jaxpr/dot_general | solution.py:32
  206.5 0.0 all-reduce.3.cloned.1.call-update
  206.5 0.2 all-reduce.5.cloned.1.call-start
  206.7 77.0 %all-reduce.3.cloned.1.call-done = f32[4096,128]{1,0:T(8,128)} async-done(((f32[4096,128]{1,0:T(8,128)}), f32[4096,128]{1,0:T(8,128)}) %all-reduce.3.cloned.1.call-update) | async-done | bytes 2097168 | tf_op jit(solution)/shard_map/psum | solution.py:36
  283.8 1.0 constant_dynamic-slice_fusion.1
  284.8 0.0 copy-start
  284.8 1.2 fusion.14
  286.0 0.0 all-reduce.5.cloned.1.call-update
  286.0 144.6 %all-reduce.5.cloned.1.call-done = f32[128,128]{0,1:T(8,128)} async-done(((f32[128,128]{0,1:T(8,128)}), f32[128,128]{0,1:T(8,128)}) %all-reduce.5.cloned.1.call-update) | async-done | bytes 65552 | tf_op jit(solution)/shard_map/psum | solution.py:42
  430.6 0.9 copy.5
  431.5 0.9 fusion.13
  432.4 11.7 %cholesky.16 = f32[128,128]{1,0:T(8,128)S(1)} custom-call(f32[128,128]{1,0:T(8,128)S(1)} %fusion.13), custom_call_target="Cholesky" | custom-call | tf_op jit(solution)/shard_map/jit(cholesky)/cholesky | solution.py:43
  444.1 0.6 compare_reduce_fusion
  444.8 0.7 fusion.11
  445.4 9.8 %custom-call.7 = f32[1,128,128]{1,2,0:T(8,128)S(1)} custom-call(f32[1,128,128]{2,1,0:T(8,128)S(1)} %fusion.11), custom_call_target="InvertDiagBlocksLowerTriangular" | custom-call | tf_op jit(solution)/shard_map/jit(_solve_triangular)/triangular_solve | solution.py:44
  455.2 1.1 convolution_multiply_fusion
  456.3 0.0 copy-done
  (11 shorter events, 0.1 us)
Async XLA Ops:
  7.2 40.1 %all-gather.4.cloned.1.call-start = ((), (), s32[]{:S(2)}) async-start(), calls=%async_computation | async-start | bytes 1179648 | tf_op jit(solution)/shard_map/all_gather | solution.py:13
  7.9 93.5 %all-gather.6.cloned.1.call-start = ((), (), s32[]{:S(2)}) async-start(), calls=%async_computation.1 | async-start | bytes 2228224 | tf_op jit(solution)/shard_map/all_gather | solution.py:21
  8.6 141.6 %all-gather.8.cloned.1.call-start = ((), (), s32[]{:S(2)}) async-start(), calls=%async_computation.2 | async-start | bytes 2228224 | tf_op jit(solution)/shard_map/all_gather | solution.py:22
  9.4 274.4 %all-reduce.3.cloned.1.call-start = ((), (), s32[]{:S(2)}) async-start(), calls=%async_computation.3 | async-start | bytes 4194304 | tf_op jit(solution)/shard_map/psum | solution.py:36
  101.4 48.8 %copy-start.1 = (bf16[8192,128]{1,0:T(8,128)(2,1)S(1)}, bf16[8192,128]{1,0:T(8,128)(2,1)}, u32[]{:S(2)}) copy-start(bf16[8192,128]{1,0:T(8,128)(2,1)} %all-gather.6.cloned.1.call-done) | copy-start | bytes 6291460
  206.5 224.1 %all-reduce.5.cloned.1.call-start = ((), (), s32[]{:S(2)}) async-start(), calls=%async_computation.4 | async-start | bytes 131072 | tf_op jit(solution)/shard_map/psum | solution.py:42
  284.8 171.6 %copy-start = (f32[512,128]{1,0:T(8,128)}, f32[512,128]{1,0:T(8,128)S(1)}, u32[]{:S(2)}) copy-start(f32[512,128]{1,0:T(8,128)S(1)} %constant_dynamic-slice_fusion.1) | copy-start | bytes 786436
Sparse Core Ops, SparseCore 0:
  9.6 37.5 all-gather.3
  49.7 51.6 all-gather.5
  103.9 46.2 all-gather.7
  206.6 77.1 all-reduce.2
  289.0 141.5 all-reduce.4
where the time goes:
time: 463 us
  waiting for transfers between devices  360 us (78%)
  matrix products  58.5 us (13%)
  other arithmetic  28.4 us (6%)
  between operations  13.9 us (3%)
    psum x1, waiting for transfers between devices, shards(): gram = lax.psum(gram_part, ('row', 'col'))  145 us
    psum x1, waiting for transfers between devices, shards(): total = lax.psum(partial_rows, 'col')  77 us
    dot_general x8, matrix products, one_block(): return jnp.dot(kernel, col_probe, preferred_element_type=jnp.float32)  56.2 us
    all_gather x1, waiting for transfers between devices, shards(): col_pts = lax.all_gather(points, 'row', axis=0, tiled=True)  52.3 us
    all_gather x1, waiting for transfers between devices, shards(): col_probe = lax.all_gather(probes, 'row', axis=0, tiled=True)  45.9 us
    all_gather x1, waiting for transfers between devices, shards(): row_pts = lax.all_gather(points, 'col', axis=0, tiled=True)  37.8 us
    another operation x3, other arithmetic, shards(): lower = jnp.linalg.cholesky(gram)  12.4 us
    another operation x2, other arithmetic, shards(): solved = jax.scipy.linalg.solve_triangular(lower, own_rows.T, lower=True)  10.5 us
  transfers between devices with their start and end apart: 5, of which 5 were waited for; matrix products, arithmetic and copies ran while one was open for 1% of the time, Pallas kernels for 0%

commit v1 on v0

--- a/solution.py
+++ b/solution.py
@@ -39,7 +39,9 @@
     gram_part = jnp.dot(
         own_rows.T, own_rows, precision=lax.Precision.HIGHEST, preferred_element_type=jnp.float32
     )
-    gram = lax.psum(gram_part, ("row", "col"))
+    gram = gram_part
+    for dev_j in ("row", "col"):
+        gram = lax.psum(gram, dev_j)
     lower = jnp.linalg.cholesky(gram)
     solved = jax.scipy.linalg.solve_triangular(lower, own_rows.T, lower=True)
     basis = solved.T * math.sqrt(all_points)

time: 463 us -> 526 us (1.14)
  waiting for transfers between devices: 360 us -> 418 us
    psum x1 -> x2, waiting for transfers between devices: 145 us -> 202 us  [shards(): gram = lax.psum(gram, dev_j)]
  transfers between devices with their start and end apart: 5 -> 6, of which waited for: 5 -> 6; matrix products, arithmetic and copies ran while one was open for 1% -> 1% of each run, Pallas kernels for 0% -> 0%
where the time goes in v1:
time: 526 us; the launch traced here: 521 us
  waiting for transfers between devices  418 us (79%)
  matrix products  58.5 us (11%)
  other arithmetic  28.4 us (5%)
  between operations  14.2 us (3%)
    psum x2, waiting for transfers between devices, shards(): gram = lax.psum(gram, dev_j)  202 us
    psum x1, waiting for transfers between devices, shards(): total = lax.psum(partial_rows, 'col')  77.2 us
    dot_general x8, matrix products, one_block(): return jnp.dot(kernel, col_probe, preferred_element_type=jnp.float32)  56.2 us
    all_gather x1, waiting for transfers between devices, shards(): col_pts = lax.all_gather(points, 'row', axis=0, tiled=True)  52.3 us
    all_gather x1, waiting for transfers between devices, shards(): col_probe = lax.all_gather(probes, 'row', axis=0, tiled=True)  45.9 us
    all_gather x1, waiting for transfers between devices, shards(): row_pts = lax.all_gather(points, 'col', axis=0, tiled=True)  37.8 us
    another operation x3, other arithmetic, shards(): lower = jnp.linalg.cholesky(gram)  12.4 us
  transfers between devices with their start and end apart: 6, of which 6 were waited for; matrix products, arithmetic and copies ran while one was open for 1% of the time, Pallas kernels for 0%

profile of v1, /device:TPU:1, one launch (start us, length us, event | category | flops | bytes accessed | tf_op | source)
XLA Modules:
  0.0 521.1 jit_solution(3104737081972666881)
XLA Ops:
  7.2 0.0 all-gather.4.cloned.1.call-start
  7.2 0.7 all-gather.4.cloned.1.call-update
  7.9 0.0 all-gather.6.cloned.1.call-start
  7.9 0.7 all-gather.6.cloned.1.call-update
  8.6 0.0 all-gather.8.cloned.1.call-start
  8.7 0.7 all-gather.8.cloned.1.call-update
  9.4 0.0 all-reduce.4.cloned.1.call-start
  9.4 37.8 %all-gather.4.cloned.1.call-done = bf16[4096,128]{1,0:T(8,128)(2,1)} async-done(((bf16[512,128]{1,0:T(8,128)(2,1)}), bf16[4096,128]{1,0:T(8,128)(2,1)}) %all-gather.4.cloned.1.call-update) | async-done | bytes 1048592 | tf_op jit(solution)/shard_map/all_gather | solution.py:13
  47.2 1.8 multiply_reduce_fusion.1
  49.1 52.3 %all-gather.6.cloned.1.call-done = bf16[8192,128]{1,0:T(8,128)(2,1)} async-done(((bf16[512,128]{1,0:T(8,128)(2,1)}), bf16[8192,128]{1,0:T(8,128)(2,1)}) %all-gather.6.cloned.1.call-update) | async-done | bytes 2097168 | tf_op jit(solution)/shard_map/all_gather | solution.py:21
  101.4 0.0 copy-start.1
  101.4 2.9 multiply_reduce_fusion
  104.3 45.9 %all-gather.8.cloned.1.call-done = bf16[8192,128]{1,0:T(8,128)(2,1)} async-done(((bf16[512,128]{1,0:T(8,128)(2,1)}), bf16[8192,128]{1,0:T(8,128)(2,1)}) %all-gather.8.cloned.1.call-update) | async-done | bytes 2097168 | tf_op jit(solution)/shard_map/all_gather | solution.py:22
  150.2 0.0 copy-done.1
  150.2 56.3 %while.10 = (s32[]{:T(128)}, f32[8,512,128]{2,1,0:T(8,128)}, f32[8,512]{1,0:T(8,128)S(1)}, f32[8192]{0:T(1024)S(1)}, bf16[8,512,128]{2,1,0:T(8,128)(2,1)}, /*ind...) while((s32[]{:T(128)}, f32[8,512,128]{2,1,0:T(8,128)}, f32[8,512]{1,0:T(8,128)S(1)}, ...), condition=%wide.region_3.4_spmd, body=%wide.region_2.3_spmd.sunk | while | flops 2168455168 | bytes 4627545 | solution.py:34
  150.2 7.0 %fusion.27 = f32[8,512,128]{2,1,0:T(8,128)} fusion(f32[8,512,128]{2,1,0:T(8,128)} %get-tuple-element.106, s32[]{:T(128)} %get-tuple-element.105, bf16[8192,128]{1,0:T(8,128)(2,1)} %get-tuple-element.119, bf16[8192,128]{1,0:T(8,128)(2,1)S(1)} %get-tuple-element.118, f32[8192]{0:T(1024)S(1)} %get-tuple-element.116, f32[512]{0:T(512)S(1)} %bitcast.37, ...), kind=kOutput, calls=%fused_computation.3.clone.1 | convolution fusion | flops 2168455168 | bytes 4623360 | tf_op jit(solution)/shard_map/while/body/eval_jaxpr/dot_general | solution.py:32
  157.2 7.0 %fusion.27 = f32[8,512,128]{2,1,0:T(8,128)} fusion(f32[8,512,128]{2,1,0:T(8,128)} %get-tuple-element.106, s32[]{:T(128)} %get-tuple-element.105, bf16[8192,128]{1,0:T(8,128)(2,1)} %get-tuple-element.119, bf16[8192,128]{1,0:T(8,128)(2,1)S(1)} %get-tuple-element.118, f32[8192]{0:T(1024)S(1)} %get-tuple-element.116, f32[512]{0:T(512)S(1)} %bitcast.37, ...), kind=kOutput, calls=%fused_computation.3.clone.1 | convolution fusion | flops 2168455168 | bytes 4623360 | tf_op jit(solution)/shard_map/while/body/eval_jaxpr/dot_general | solution.py:32
  164.3 7.0 %fusion.27 = f32[8,512,128]{2,1,0:T(8,128)} fusion(f32[8,512,128]{2,1,0:T(8,128)} %get-tuple-element.106, s32[]{:T(128)} %get-tuple-element.105, bf16[8192,128]{1,0:T(8,128)(2,1)} %get-tuple-element.119, bf16[8192,128]{1,0:T(8,128)(2,1)S(1)} %get-tuple-element.118, f32[8192]{0:T(1024)S(1)} %get-tuple-element.116, f32[512]{0:T(512)S(1)} %bitcast.37, ...), kind=kOutput, calls=%fused_computation.3.clone.1 | convolution fusion | flops 2168455168 | bytes 4623360 | tf_op jit(solution)/shard_map/while/body/eval_jaxpr/dot_general | solution.py:32
  171.3 7.0 %fusion.27 = f32[8,512,128]{2,1,0:T(8,128)} fusion(f32[8,512,128]{2,1,0:T(8,128)} %get-tuple-element.106, s32[]{:T(128)} %get-tuple-element.105, bf16[8192,128]{1,0:T(8,128)(2,1)} %get-tuple-element.119, bf16[8192,128]{1,0:T(8,128)(2,1)S(1)} %get-tuple-element.118, f32[8192]{0:T(1024)S(1)} %get-tuple-element.116, f32[512]{0:T(512)S(1)} %bitcast.37, ...), kind=kOutput, calls=%fused_computation.3.clone.1 | convolution fusion | flops 2168455168 | bytes 4623360 | tf_op jit(solution)/shard_map/while/body/eval_jaxpr/dot_general | solution.py:32
  178.3 7.0 %fusion.27 = f32[8,512,128]{2,1,0:T(8,128)} fusion(f32[8,512,128]{2,1,0:T(8,128)} %get-tuple-element.106, s32[]{:T(128)} %get-tuple-element.105, bf16[8192,128]{1,0:T(8,128)(2,1)} %get-tuple-element.119, bf16[8192,128]{1,0:T(8,128)(2,1)S(1)} %get-tuple-element.118, f32[8192]{0:T(1024)S(1)} %get-tuple-element.116, f32[512]{0:T(512)S(1)} %bitcast.37, ...), kind=kOutput, calls=%fused_computation.3.clone.1 | convolution fusion | flops 2168455168 | bytes 4623360 | tf_op jit(solution)/shard_map/while/body/eval_jaxpr/dot_general | solution.py:32
  185.4 7.0 %fusion.27 = f32[8,512,128]{2,1,0:T(8,128)} fusion(f32[8,512,128]{2,1,0:T(8,128)} %get-tuple-element.106, s32[]{:T(128)} %get-tuple-element.105, bf16[8192,128]{1,0:T(8,128)(2,1)} %get-tuple-element.119, bf16[8192,128]{1,0:T(8,128)(2,1)S(1)} %get-tuple-element.118, f32[8192]{0:T(1024)S(1)} %get-tuple-element.116, f32[512]{0:T(512)S(1)} %bitcast.37, ...), kind=kOutput, calls=%fused_computation.3.clone.1 | convolution fusion | flops 2168455168 | bytes 4623360 | tf_op jit(solution)/shard_map/while/body/eval_jaxpr/dot_general | solution.py:32
  192.4 7.0 %fusion.27 = f32[8,512,128]{2,1,0:T(8,128)} fusion(f32[8,512,128]{2,1,0:T(8,128)} %get-tuple-element.106, s32[]{:T(128)} %get-tuple-element.105, bf16[8192,128]{1,0:T(8,128)(2,1)} %get-tuple-element.119, bf16[8192,128]{1,0:T(8,128)(2,1)S(1)} %get-tuple-element.118, f32[8192]{0:T(1024)S(1)} %get-tuple-element.116, f32[512]{0:T(512)S(1)} %bitcast.37, ...), kind=kOutput, calls=%fused_computation.3.clone.1 | convolution fusion | flops 2168455168 | bytes 4623360 | tf_op jit(solution)/shard_map/while/body/eval_jaxpr/dot_general | solution.py:32
  199.4 7.0 %fusion.27 = f32[8,512,128]{2,1,0:T(8,128)} fusion(f32[8,512,128]{2,1,0:T(8,128)} %get-tuple-element.106, s32[]{:T(128)} %get-tuple-element.105, bf16[8192,128]{1,0:T(8,128)(2,1)} %get-tuple-element.119, bf16[8192,128]{1,0:T(8,128)(2,1)S(1)} %get-tuple-element.118, f32[8192]{0:T(1024)S(1)} %get-tuple-element.116, f32[512]{0:T(512)S(1)} %bitcast.37, ...), kind=kOutput, calls=%fused_computation.3.clone.1 | convolution fusion | flops 2168455168 | bytes 4623360 | tf_op jit(solution)/shard_map/while/body/eval_jaxpr/dot_general | solution.py:32
  206.5 0.0 all-reduce.4.cloned.1.call-update
  206.5 0.0 all-reduce.6.cloned.1.call-start
  206.6 77.2 %all-reduce.4.cloned.1.call-done = f32[4096,128]{1,0:T(8,128)} async-done(((f32[4096,128]{1,0:T(8,128)}), f32[4096,128]{1,0:T(8,128)}) %all-reduce.4.cloned.1.call-update) | async-done | bytes 2097168 | tf_op jit(solution)/shard_map/psum | solution.py:36
  283.8 1.0 constant_dynamic-slice_fusion.1
  284.8 0.0 copy-start
  284.8 1.2 fusion.14
  286.0 0.0 all-reduce.6.cloned.1.call-update
  286.0 0.2 all-reduce.8.cloned.1.call-start
  286.2 130.2 %all-reduce.6.cloned.1.call-done = f32[128,128]{0,1:T(8,128)} async-done(((f32[128,128]{0,1:T(8,128)}), f32[128,128]{0,1:T(8,128)}) %all-reduce.6.cloned.1.call-update) | async-done | bytes 65552 | tf_op jit(solution)/shard_map/psum | solution.py:44
  416.4 0.0 all-reduce.8.cloned.1.call-update
  416.5 72.0 %all-reduce.8.cloned.1.call-done = f32[128,128]{0,1:T(8,128)} async-done(((f32[128,128]{0,1:T(8,128)}), f32[128,128]{0,1:T(8,128)}) %all-reduce.8.cloned.1.call-update) | async-done | bytes 65552 | tf_op jit(solution)/shard_map/psum | solution.py:44
  488.5 0.9 copy.5
  489.4 0.9 fusion.13
  490.3 11.7 %cholesky.16 = f32[128,128]{1,0:T(8,128)S(1)} custom-call(f32[128,128]{1,0:T(8,128)S(1)} %fusion.13), custom_call_target="Cholesky" | custom-call | tf_op jit(solution)/shard_map/jit(cholesky)/cholesky | solution.py:45
  502.0 0.6 compare_reduce_fusion
  502.7 0.7 fusion.11
  503.3 9.8 %custom-call.7 = f32[1,128,128]{1,2,0:T(8,128)S(1)} custom-call(f32[1,128,128]{2,1,0:T(8,128)S(1)} %fusion.11), custom_call_target="InvertDiagBlocksLowerTriangular" | custom-call | tf_op jit(solution)/shard_map/jit(_solve_triangular)/triangular_solve | solution.py:46
  513.1 1.1 convolution_multiply_fusion
  514.2 0.0 copy-done
  (11 shorter events, 0.1 us)
Async XLA Ops:
  7.2 40.1 %all-gather.4.cloned.1.call-start = ((), (), s32[]{:S(2)}) async-start(), calls=%async_computation | async-start | bytes 1179648 | tf_op jit(solution)/shard_map/all_gather | solution.py:13
  7.9 93.5 %all-gather.6.cloned.1.call-start = ((), (), s32[]{:S(2)}) async-start(), calls=%async_computation.1 | async-start | bytes 2228224 | tf_op jit(solution)/shard_map/all_gather | solution.py:21
  8.6 141.6 %all-gather.8.cloned.1.call-start = ((), (), s32[]{:S(2)}) async-start(), calls=%async_computation.2 | async-start | bytes 2228224 | tf_op jit(solution)/shard_map/all_gather | solution.py:22
  9.4 274.4 %all-reduce.4.cloned.1.call-start = ((), (), s32[]{:S(2)}) async-start(), calls=%async_computation.3 | async-start | bytes 4194304 | tf_op jit(solution)/shard_map/psum | solution.py:36
  101.4 48.8 %copy-start.1 = (bf16[8192,128]{1,0:T(8,128)(2,1)S(1)}, bf16[8192,128]{1,0:T(8,128)(2,1)}, u32[]{:S(2)}) copy-start(bf16[8192,128]{1,0:T(8,128)(2,1)} %all-gather.6.cloned.1.call-done) | copy-start | bytes 6291460
  206.5 209.9 %all-reduce.6.cloned.1.call-start = ((), (), s32[]{:S(2)}) async-start(), calls=%async_computation.4 | async-start | bytes 131072 | tf_op jit(solution)/shard_map/psum | solution.py:44
  284.8 229.5 %copy-start = (f32[512,128]{1,0:T(8,128)}, f32[512,128]{1,0:T(8,128)S(1)}, u32[]{:S(2)}) copy-start(f32[512,128]{1,0:T(8,128)S(1)} %constant_dynamic-slice_fusion.1) | copy-start | bytes 786436
  286.0 202.5 %all-reduce.8.cloned.1.call-start = ((), (), s32[]{:S(2)}) async-start(), calls=%async_computation.5 | async-start | bytes 131072 | tf_op jit(solution)/shard_map/psum | solution.py:44
Sparse Core Ops, SparseCore 0:
  9.6 37.5 all-gather.3
  49.7 51.6 all-gather.5
  103.9 46.2 all-gather.7
  206.6 77.1 all-reduce.3
  286.7 129.7 all-reduce.5
  418.9 69.5 all-reduce.7
